TPU v7x, 32 devices: a whole 2x2x4 slice. The times are simulated.
32 devices in a mesh: dp: 4 (over y, x), tp: 8 (over z, core).
Axes of the slice: x: 2, y: 2, z: 4, core: 2. Of those that a mesh axis runs over, the one named last changes fastest.
Arguments:
- hidden_in: bfloat16 [4, 32, 4096], P(None, 'dp'), may hold values from -6 to 6
- pre_gain: float32 [4096], replicated, may hold values from 0.25 to 1.75
- w_zx: bfloat16 [4096, 2, 8192], P(None, None, 'tp'), may hold values from -0.09375 to 0.09375
- zx_codes: bfloat16 [4096, 2, 8192], P(('dp', 'tp')), may hold values from -4 to 4
- zx_exponents: int32 [32, 2, 64], P('dp', None, 'tp'), may hold values from -9 to -6
- w_bc: bfloat16 [4096, 2048], P(None, 'tp'), may hold values from -0.09375 to 0.09375
- w_dt: bfloat16 [4096, 128], P(None, 'tp'), may hold values from -0.09375 to 0.09375
- conv_x: float32 [5, 8192], P(None, 'tp'), may hold values from -0.6 to 0.6
- conv_bc: float32 [5, 2048], P(None, 'tp'), may hold values from -0.6 to 0.6
- dt_bias: float32 [128], P('tp'), may hold values from -2 to 0.5
- decay_rate: float32 [128], P('tp'), may hold values from 0.05 to 2
- skip_gain: float32 [128], P('tp'), may hold values from 0.5 to 1.5
- conv_state_x: bfloat16 [32, 3, 8192], P('dp', None, 'tp'), may hold values from -6 to 6
- conv_state_bc: bfloat16 [32, 3, 2048], P('dp', None, 'tp'), may hold values from -6 to 6
- ssm_state: float32 [32, 128, 64, 256], P('dp', 'tp'), may hold values from -6 to 6
- norm_gain: float32 [8192], P('tp'), may hold values from 0.25 to 1.75
- w_out: bfloat16 [8192, 4096], P('tp'), may hold values from -0.0625 to 0.0625
- out_codes: bfloat16 [8192, 4096], P('tp', 'dp'), may hold values from -4 to 4
- out_exponents: int32 [64, 32], P('tp', 'dp'), may hold values from -7 to -4
Outputs:
- mixed: bfloat16 [4, 32, 4096], P(None, 'dp', 'tp')
- final_state: float32 [32, 128, 64, 256], P('dp', 'tp')
All inputs are finite; a program needn't handle non-finite values.
Results may differ from a plain program's by a relative error of at most 0.014.
Values may be sent and summed in bfloat16 or wider, within the bound.
A program may use at most 192 MiB of HBM per device.

v0:
```python
import jax
import jax.numpy as jnp
from jax import lax
from jax.sharding import PartitionSpec as P

D = 4096
H = 128
G = 4
BLK = 128
STEPS = 4
DI = 8192
EPS = 1e-05


def decode_pairs(codes, exponents, block):
    rows, pair, cols = codes.shape
    blocked = codes.astype(jnp.float32).reshape(rows // block, block, pair, cols // block, block)
    scales = jnp.exp2(exponents.astype(jnp.float32))
    return (blocked * scales[:, None, :, :, None]).reshape(rows, pair, cols)


def decode_matrix(codes, exponents, block):
    rows, cols = codes.shape
    blocked = codes.astype(jnp.float32).reshape(rows // block, block, cols // block, block)
    scales = jnp.exp2(exponents.astype(jnp.float32))
    return (blocked * scales[:, None, :, None]).reshape(rows, cols)


def conv_step(history, fresh, params):
    window = jnp.concatenate([history, fresh[:, None, :]], axis=1)
    mixed = jnp.sum(window * params[:4][None], axis=1) + params[4]
    return (jax.nn.silu(mixed), window[:, 1:])


def body(
    hidden_in,
    pre_gain,
    w_zx,
    zx_codes,
    zx_exponents,
    w_bc,
    w_dt,
    conv_x,
    conv_bc,
    dt_bias,
    decay_rate,
    skip_gain,
    conv_state_x,
    conv_state_bc,
    ssm_state,
    norm_gain,
    w_out,
    out_codes,
    out_exponents,
):
    slot = lax.axis_index("tp")
    tp_count = lax.axis_size("tp")
    traded = lax.all_to_all(zx_codes, "tp", split_axis=2, concat_axis=0, tiled=True)
    zx_delta = decode_pairs(traded, zx_exponents, BLK)
    local_cols = traded.shape[2]
    gathered = lax.all_gather(zx_delta.astype(jnp.bfloat16), "dp", axis=0, tiled=True)
    zx_weights = (
        (w_zx.astype(jnp.float32) + gathered.astype(jnp.float32))
        .astype(jnp.bfloat16)
        .reshape(D, 2 * local_cols)
    )
    out_piece = decode_matrix(out_codes, out_exponents, BLK).astype(jnp.bfloat16)
    out_full = lax.all_gather(out_piece, "dp", axis=1, tiled=True)
    new_out = (w_out.astype(jnp.float32) + out_full.astype(jnp.float32)).astype(jnp.bfloat16)
    heads_here = ssm_state.shape[1]
    states_n = ssm_state.shape[3]
    group = slot * heads_here // (H // G)
    group_mask = (jnp.arange(G) == group).astype(jnp.float32)
    history_x = conv_state_x.astype(jnp.float32)
    history_bc = conv_state_bc.astype(jnp.float32)
    state = ssm_state
    results = []
    carried = None
    for step in range(STEPS):
        x = hidden_in[step].astype(jnp.float32)
        if step > 0:
            x = x + carried.astype(jnp.float32)
        rows = x.shape[0]
        normed = (x * lax.rsqrt(jnp.mean(x * x, -1, keepdims=True) + EPS) * pre_gain).astype(
            jnp.bfloat16
        )
        zx = jnp.dot(normed, zx_weights, preferred_element_type=jnp.float32)
        zx = zx.reshape(rows, 2, local_cols)
        gate = zx[:, 0]
        inner = zx[:, 1]
        bc_raw = jnp.dot(normed, w_bc, preferred_element_type=jnp.float32)
        dt_raw = jnp.dot(normed, w_dt, preferred_element_type=jnp.float32)
        conv_inner, history_x = conv_step(history_x, inner, conv_x)
        conv_piece, history_bc = conv_step(history_bc, bc_raw, conv_bc)
        bc_all = lax.all_gather(conv_piece, "tp", axis=1, tiled=True)
        b_group = lax.dynamic_slice_in_dim(bc_all, group * states_n, states_n, 1)
        c_group = lax.dynamic_slice_in_dim(bc_all, G * states_n + group * states_n, states_n, 1)
        step_size = jax.nn.softplus(dt_raw + dt_bias)
        decay = jnp.exp(-step_size * decay_rate)
        inner_heads = conv_inner.reshape(rows, heads_here, -1)
        state = (
            decay[:, :, None, None] * state
            + (step_size[:, :, None] * inner_heads)[:, :, :, None] * b_group[:, None, None, :]
        )
        read = (
            jnp.einsum("rhpn,rn->rhp", state, c_group, precision=lax.Precision.HIGHEST)
            + skip_gain[:, None] * inner_heads
        )
        gated = read.reshape(rows, local_cols) * jax.nn.silu(gate)
        squares = jnp.sum(gated * gated, -1)
        totals = lax.psum(squares[:, None] * group_mask, "tp")
        mean_sq = jnp.sum(totals * group_mask, -1) / (DI // G)
        scaled = (gated * lax.rsqrt(mean_sq + EPS)[:, None] * norm_gain).astype(jnp.bfloat16)
        partial_value = jnp.dot(scaled, new_out, preferred_element_type=jnp.float32)
        whole = lax.psum(partial_value, "tp").astype(jnp.bfloat16)
        width = partial_value.shape[1] // tp_count
        results.append(lax.dynamic_slice_in_dim(whole, slot * width, width, 1))
        carried = whole
    return (jnp.stack(results), state)


def solution(mesh):
    return jax.shard_map(
        body,
        mesh=mesh,
        in_specs=(
            P(None, "dp", None),
            P(),
            P(None, None, "tp"),
            P(("dp", "tp"), None, None),
            P("dp", None, "tp"),
            P(None, "tp"),
            P(None, "tp"),
            P(None, "tp"),
            P(None, "tp"),
            P("tp"),
            P("tp"),
            P("tp"),
            P("dp", None, "tp"),
            P("dp", None, "tp"),
            P("dp", "tp", None, None),
            P("tp"),
            P("tp", None),
            P("tp", "dp"),
            P("tp", "dp"),
        ),
        out_specs=(P(None, "dp", "tp"), P("dp", "tp", None, None)),
        check_vma=False,
    )
```

profile of v0, /device:TPU:0, one launch (start us, length us, event | category | flops | bytes accessed | tf_op | source)
XLA Modules:
  0.0 712.7 jit_solution(7525767807919478908)
XLA Ops:
  7.2 0.8 multiply_exponential_fusion.4
  8.1 0.3 mul.639
  8.4 4.1 fusion.3
  12.6 15.0 %copy.29 = bf16[128,2,8192]{0,1,2:T(2,128)(2,1)} copy(bf16[128,2,8192]{2,1,0:T(2,128)(2,1)} %param.22) | data formatting | bytes 8388608 | tf_op args[3]
  27.6 6.4 all-to-all-start
  34.1 4.0 mul.609
  38.1 10.8 %mul.610 = f32[1024,2,1024]{2,1,0:T(2,128)} reshape(f32[8,128,2,8,128]{4,3,2,1,0:T(8,128)} %mul.609) | data formatting | bytes 16777216 | tf_op jit(solution)/shard_map/mul | solution.py:19
  48.8 79.2 %all-to-all-done = bf16[128,2,8192]{0,1,2:T(2,128)(2,1)} async-done(((bf16[128,2,8192]{0,1,2:T(2,128)(2,1)}), bf16[128,2,8192]{0,1,2:T(2,128)(2,1)}, u32[]{:S(2)}, u32[]{:S(2)}) %all-to-all-start) | async-done | bytes 4194336 | tf_op jit(solution)/shard_map/all_to_all | solution.py:58
  128.1 8.5 %convert_bitcast_fusion = f32[8,128,2,1024]{1,2,3,0:T(2,128)} fusion(bf16[128,2,8,1024]{0,1,3,2:T(2,128)(2,1)} %bitcast.39), kind=kLoop, calls=%fused_computation.2 | loop fusion | flops 2097152 | bytes 12582912 | tf_op jit(solution)/shard_map/convert_element_type | solution.py:17
  136.5 17.1 %copy.30 = f32[8,128,2,1024]{3,2,1,0:T(2,128)} copy(f32[8,128,2,1024]{1,2,3,0:T(2,128)} %convert_bitcast_fusion) | data formatting | bytes 16777216 | tf_op jit(solution)/shard_map/convert_element_type | solution.py:17
  153.7 9.0 %fusion = bf16[1024,2,1024]{2,1,0:T(2,128)(2,1)} fusion(f32[1024,2,1024]{2,1,0:T(2,128)} %mul.610, f32[8,128,2,1024]{3,2,1,0:T(2,128)} %copy.30), kind=kLoop, calls=%fused_computation.4 | loop fusion | flops 4194304 | bytes 20971520 | tf_op jit(solution)/shard_map/convert_element_type | solution.py:61
  163.0 0.1 fusion.13
  163.2 0.4 convolution_bitcast_fusion.3
  163.6 14.2 %all_gather.19 = f32[8,2048]{1,0:T(8,128)S(1)} all-gather(f32[8,256]{1,0:T(8,128)S(1)} %divide_multiply_fusion.7), channel_id=1, replica_groups=mesh['dp'=4,'tp'=8] {'tp'}, dimensions={1}, use_global_device_ids=true | all-gather | bytes 73728 | tf_op jit(solution)/shard_map/all_gather | solution.py:95
  177.8 0.2 multiply_exponential_fusion.5
  178.1 10.1 %add_convert_fusion.1 = bf16[1024,4096]{1,0:T(8,128)(2,1)} fusion(bf16[1024,4096]{1,0:T(8,128)(2,1)} %all-gather.5.cloned.1.call-done, bf16[1024,4096]{1,0:T(8,128)(2,1)} %param.35), kind=kLoop, calls=%fused_computation.1 | loop fusion | flops 16777216 | bytes 25165824 | tf_op jit(solution)/shard_map/convert_element_type | solution.py:69
  188.2 131.0 %all-gather.3.cloned.1.call-done = bf16[4096,2,1024]{2,1,0:T(2,128)(2,1)} async-done(((bf16[1024,2,1024]{2,1,0:T(2,128)(2,1)}), bf16[4096,2,1024]{2,1,0:T(2,128)(2,1)}) %all-gather.3.cloned.1.call-update) | async-done | bytes 16777232 | tf_op jit(solution)/shard_map/all_gather | solution.py:61
  319.1 19.2 %add_convert_fusion = bf16[4096,2,1024]{2,1,0:T(2,128)(2,1)S(1)} fusion(bf16[4096,2,1024]{2,1,0:T(2,128)(2,1)} %all-gather.3.cloned.1.call-done, bf16[4096,2,1024]{2,1,0:T(2,128)(2,1)} %param.21), kind=kLoop, calls=%fused_computation | loop fusion | flops 33554432 | bytes 50331648 | tf_op jit(solution)/shard_map/convert_element_type | solution.py:64
  338.3 9.3 %copy.40 = bf16[512,8,2,1024]{3,1,2,0:T(8,128)(2,1)} copy(bf16[512,8,2,1024]{3,2,1,0:T(2,128)(2,1)S(1)} %bitcast.210) | data formatting | bytes 33554432
  347.6 20.7 %copy.31 = bf16[2048,4096]{1,0:T(8,128)(2,1)} copy(bf16[2048,4096]{0,1:T(8,128)(2,1)} %bitcast.211) | data formatting | bytes 33554432 | tf_op jit(solution)/shard_map/dot_general | solution.py:87
  368.3 10.2 %fusion.29 = f32[8,2,1024]{2,0,1:T(8,128)S(1)} fusion(bf16[2,1024,4096]{2,1,0:T(8,128)(2,1)} %bitcast.206, f32[4096]{0:T(1024)S(1)} %copy-done.5, f32[8]{0:T(128)S(1)} %add_rsqrt_fusion.7, bf16[4,8,4096]{2,1,0:T(8,128)(2,1)S(1)} %copy-done.2), kind=kOutput, calls=%fused_computation.67 | convolution fusion | flops 134348800 | bytes 16925184 | tf_op jit(solution)/shard_map/dot_general | solution.py:87
  378.8 13.1 %fusion.1 = f32[8,1,16,64]{3,1,2,0:T(1,128)S(1)} fusion(f32[8,16,64,256]{3,2,1,0:T(8,128)} %param.33, f32[8,256]{1,0:T(8,128)S(1)} %get-tuple-element.23, f32[8,16,64]{2,1,0:T(8,128)S(1)} %broadcast_multiply_fusion.3, f32[8,16]{1,0:T(8,128)S(1)} %get-tuple-element.26, f32[8,256,1,1]{1,0,2,3:T(8,128)S(1)} %get-tuple-element.22), kind=kOutput, calls=%fused_computation.9 | convolution fusion | flops 31457280 | bytes 8471040 | tf_op jit(solution)/shard_map/rhpn,rn->rhp/dot_general | solution.py:106
  391.9 0.2 multiply_reduce_fusion.6
  392.2 16.4 %psum.56 = f32[8,4]{0,1:T(4,128)S(1)} all-reduce(f32[8,4]{0,1:T(4,128)S(1)} %broadcast_multiply_fusion.7), channel_id=1, replica_groups=mesh['dp'=4,'tp'=8] {'tp'}, use_global_device_ids=true, to_apply=%region_4.5 | all-reduce | flops 32 | bytes 256 | tf_op jit(solution)/shard_map/psum | solution.py:111
  408.8 4.6 fusion.84
  413.4 27.1 %all-reduce.4 = bf16[8,4096]{1,0:T(8,128)(2,1)S(1)} all-reduce(f32[8,4096]{1,0:T(8,128)S(1)} %fusion.84), channel_id=1, replica_groups=mesh['dp'=4,'tp'=8] {'tp'}, use_global_device_ids=true, to_apply=%region_6.7 | all-reduce | flops 32768 | bytes 196608 | tf_op jit(solution)/shard_map/psum | solution.py:115
  440.5 0.1 multiply_reduce_fusion.2
  440.7 0.1 multiply_convert_fusion.2
  440.8 10.2 %fusion.35 = f32[8,2,1024]{2,0,1:T(8,128)S(1)} fusion(bf16[2,1024,4096]{2,1,0:T(8,128)(2,1)} %bitcast.207, bf16[8,4096]{1,0:T(8,128)(2,1)S(1)} %multiply_convert_fusion.2), kind=kOutput, calls=%fused_computation.72 | convolution fusion | flops 134217728 | bytes 16908288 | tf_op jit(solution)/shard_map/dot_general | solution.py:87
  451.0 0.2 multiply_exponential_fusion.3
  451.2 0.4 convolution_bitcast_fusion.2
  451.7 14.0 %all_gather.21 = f32[8,2048]{1,0:T(8,128)S(1)} all-gather(f32[8,256]{1,0:T(8,128)S(1)} %divide_multiply_fusion.6), channel_id=1, replica_groups=mesh['dp'=4,'tp'=8] {'tp'}, dimensions={1}, use_global_device_ids=true | all-gather | bytes 73728 | tf_op jit(solution)/shard_map/all_gather | solution.py:95
  465.9 13.7 %fusion.10 = f32[8,1,16,64]{3,1,2,0:T(1,128)S(1)} fusion(f32[8,16,64,256]{3,2,1,0:T(8,128)} %param.33, f32[8,256]{1,0:T(8,128)S(1)} %get-tuple-element.19, f32[8,16,64]{2,1,0:T(8,128)S(1)} %broadcast_multiply_fusion.2, f32[8,16]{1,0:T(8,128)S(1)} %get-tuple-element.28, f32[8,256]{1,0:T(8,128)S(1)} %get-tuple-element.23, ...), kind=kOutput, calls=%fused_computation.19 | convolution fusion | flops 37748736 | bytes 8512512 | tf_op jit(solution)/shard_map/rhpn,rn->rhp/dot_general | solution.py:106
  479.5 0.2 multiply_reduce_fusion.5
  479.9 13.9 %psum.58 = f32[8,4]{0,1:T(4,128)S(1)} all-reduce(f32[8,4]{0,1:T(4,128)S(1)} %broadcast_multiply_fusion.6), channel_id=1, replica_groups=mesh['dp'=4,'tp'=8] {'tp'}, use_global_device_ids=true, to_apply=%region_11.12 | all-reduce | flops 32 | bytes 256 | tf_op jit(solution)/shard_map/psum | solution.py:111
  493.8 0.1 multiply_reduce_fusion.9
  493.9 4.6 fusion.82
  498.6 27.7 %all-reduce.5 = bf16[8,4096]{1,0:T(8,128)(2,1)S(1)} all-reduce(f32[8,4096]{1,0:T(8,128)S(1)} %fusion.82), channel_id=1, replica_groups=mesh['dp'=4,'tp'=8] {'tp'}, use_global_device_ids=true, to_apply=%region_13.14 | all-reduce | flops 32768 | bytes 196608 | tf_op jit(solution)/shard_map/psum | solution.py:115
  526.2 0.1 multiply_reduce_fusion.1
  526.4 0.1 multiply_convert_fusion.1
  526.5 10.2 %fusion.33 = f32[8,2,1024]{2,0,1:T(8,128)S(1)} fusion(bf16[2,1024,4096]{2,1,0:T(8,128)(2,1)} %bitcast.208, bf16[8,4096]{1,0:T(8,128)(2,1)S(1)} %multiply_convert_fusion.1), kind=kOutput, calls=%fused_computation.70 | convolution fusion | flops 134217728 | bytes 16908288 | tf_op jit(solution)/shard_map/dot_general | solution.py:87
  536.7 0.2 multiply_exponential_fusion.2
  536.9 0.4 convolution_bitcast_fusion.1
  537.4 14.0 %all_gather.22 = f32[8,2048]{1,0:T(8,128)S(1)} all-gather(f32[8,256]{1,0:T(8,128)S(1)} %divide_multiply_fusion.5), channel_id=1, replica_groups=mesh['dp'=4,'tp'=8] {'tp'}, dimensions={1}, use_global_device_ids=true | all-gather | bytes 73728 | tf_op jit(solution)/shard_map/all_gather | solution.py:95
  551.6 14.5 %fusion.2 = f32[8,1,16,64]{3,1,2,0:T(1,128)S(1)} fusion(f32[8,256]{1,0:T(8,128)S(1)} %get-tuple-element.15, f32[8,16,64]{2,1,0:T(8,128)S(1)} %broadcast_multiply_fusion.1, f32[8,16]{1,0:T(8,128)S(1)} %get-tuple-element.30, f32[8,16,64,256]{3,2,1,0:T(8,128)} %param.33, f32[8,256]{1,0:T(8,128)S(1)} %get-tuple-element.19, ...), kind=kOutput, calls=%fused_computation.10 | convolution fusion | flops 44040192 | bytes 8553984 | tf_op jit(solution)/shard_map/rhpn,rn->rhp/dot_general | solution.py:106
  566.1 0.2 multiply_reduce_fusion.4
  566.4 13.9 %psum.60 = f32[8,4]{0,1:T(4,128)S(1)} all-reduce(f32[8,4]{0,1:T(4,128)S(1)} %broadcast_multiply_fusion.5), channel_id=1, replica_groups=mesh['dp'=4,'tp'=8] {'tp'}, use_global_device_ids=true, to_apply=%region_18.19 | all-reduce | flops 32 | bytes 256 | tf_op jit(solution)/shard_map/psum | solution.py:111
  580.3 0.1 multiply_reduce_fusion.8
  580.5 4.6 fusion.80
  585.1 27.2 %all-reduce.6 = bf16[8,4096]{1,0:T(8,128)(2,1)S(1)} all-reduce(f32[8,4096]{1,0:T(8,128)S(1)} %fusion.80), channel_id=1, replica_groups=mesh['dp'=4,'tp'=8] {'tp'}, use_global_device_ids=true, to_apply=%region_20.21 | all-reduce | flops 32768 | bytes 196608 | tf_op jit(solution)/shard_map/psum | solution.py:115
  612.3 0.1 multiply_reduce_fusion
  612.5 0.1 multiply_convert_fusion
  612.6 10.2 %fusion.31 = f32[8,2,1024]{2,0,1:T(8,128)S(1)} fusion(bf16[2,1024,4096]{2,1,0:T(8,128)(2,1)} %bitcast.209, bf16[8,4096]{1,0:T(8,128)(2,1)S(1)} %multiply_convert_fusion), kind=kOutput, calls=%fused_computation.68 | convolution fusion | flops 134217728 | bytes 16908288 | tf_op jit(solution)/shard_map/dot_general | solution.py:87
  622.8 0.2 multiply_exponential_fusion.1
  623.0 0.4 convolution_bitcast_fusion
  623.5 14.2 %all_gather.23 = f32[8,2048]{1,0:T(8,128)S(1)} all-gather(f32[8,256]{1,0:T(8,128)S(1)} %divide_multiply_fusion.4), channel_id=1, replica_groups=mesh['dp'=4,'tp'=8] {'tp'}, dimensions={1}, use_global_device_ids=true | all-gather | bytes 73728 | tf_op jit(solution)/shard_map/all_gather | solution.py:95
  637.8 7.7 %multiply_add_fusion = f32[8,16,64,256]{3,2,1,0:T(8,128)S(1)} fusion(f32[8,256]{1,0:T(8,128)S(1)} %get-tuple-element.11, f32[8,16,64]{2,1,0:T(8,128)S(1)} %broadcast_multiply_fusion, f32[8,16]{1,0:T(8,128)S(1)} %get-tuple-element.32, f32[8,256]{1,0:T(8,128)S(1)} %get-tuple-element.15, f32[8,16,64]{2,1,0:T(8,128)S(1)} %broadcast_multiply_fusion.1, ...), kind=kLoop, calls=%fused_computation.5 | loop fusion | flops 25165824 | bytes 16943104 | tf_op jit(solution)/shard_map/add | solution.py:102
  645.5 3.4 copy-done.1
  648.9 9.8 %fusion.99 = f32[8,1,16,64]{3,1,2,0:T(1,128)S(1)} fusion(f32[8,16,64,256]{3,2,1,0:T(8,128)S(1)} %multiply_add_fusion, f32[8,256,1,1]{1,0,2,3:T(8,128)S(1)} %get-tuple-element.10), kind=kOutput, calls=%fused_computation.172 | convolution fusion | flops 25165824 | bytes 8429568 | tf_op jit(solution)/shard_map/rhpn,rn->rhp/dot_general | solution.py:106
  658.8 0.2 multiply_reduce_fusion.3
  659.1 13.9 %psum.62 = f32[8,4]{0,1:T(4,128)S(1)} all-reduce(f32[8,4]{0,1:T(4,128)S(1)} %broadcast_multiply_fusion.4), channel_id=1, replica_groups=mesh['dp'=4,'tp'=8] {'tp'}, use_global_device_ids=true, to_apply=%region_25.26 | all-reduce | flops 32 | bytes 256 | tf_op jit(solution)/shard_map/psum | solution.py:111
  673.2 4.6 fusion.78
  677.8 27.2 %all-reduce.7 = bf16[8,4096]{1,0:T(8,128)(2,1)S(1)} all-reduce(f32[8,4096]{1,0:T(8,128)S(1)} %fusion.78), channel_id=1, replica_groups=mesh['dp'=4,'tp'=8] {'tp'}, use_global_device_ids=true, to_apply=%region_27.28 | all-reduce | flops 32768 | bytes 196608 | tf_op jit(solution)/shard_map/psum | solution.py:115
  705.0 0.6 pad_maximum_fusion.6
  (101 shorter events, 2.5 us)
Async XLA Ops:
  7.2 156.0 %copy-start = (bf16[4096,256]{1,0:T(8,128)(2,1)S(1)}, bf16[4096,256]{1,0:T(8,128)(2,1)}, u32[]{:S(2)}) copy-start(bf16[4096,256]{1,0:T(8,128)(2,1)} %param.24) | copy-start | bytes 6291460
  7.2 170.9 %all-gather.5.cloned.1.call-start = ((), (), s32[]{:S(2)}) async-start(), calls=%async_computation.2 | async-start | bytes 10485760 | tf_op jit(solution)/shard_map/all_gather | solution.py:68
  12.6 21.5 %copy-start.10 = (s32[8,2,8]{2,1,0:T(2,128)S(1)}, s32[8,2,8]{2,1,0:T(2,128)}, u32[]{:S(2)}) copy-start(s32[8,2,8]{2,1,0:T(2,128)} %param.23) | copy-start | bytes 1540
  27.6 100.5 %all-to-all-start = ((bf16[128,2,8192]{0,1,2:T(2,128)(2,1)}), bf16[128,2,8192]{0,1,2:T(2,128)(2,1)}, u32[]{:S(2)}, u32[]{:S(2)}) async-start(bf16[128,2,8192]{0,1,2:T(2,128)(2,1)} %copy.29), calls=%async_computation | async-start | bytes 8388608 | tf_op jit(solution)/shard_map/all_to_all | solution.py:58
  34.0 285.2 %all-gather.3.cloned.1.call-start = ((), (), s32[]{:S(2)}) async-start(), calls=%async_computation.1 | async-start | bytes 20971520 | tf_op jit(solution)/shard_map/all_gather | solution.py:61
  153.6 9.1 %copy-start.13 = (f32[5,256]{1,0:T(8,128)S(1)}, f32[5,256]{1,0:T(8,128)}, u32[]{:S(2)}) copy-start(f32[5,256]{1,0:T(8,128)} %param.27) | copy-start | bytes 15364
  153.6 9.2 %copy-start.8 = (bf16[8,3,256]{2,0,1:T(8,128)(2,1)S(1)}, bf16[8,3,256]{2,0,1:T(8,128)(2,1)}, u32[]{:S(2)}) copy-start(bf16[8,3,256]{2,0,1:T(8,128)(2,1)} %param.32) | copy-start | bytes 36868
  153.6 9.2 %copy-start.7 = (f32[5,1024]{1,0:T(8,128)S(1)}, f32[5,1024]{1,0:T(8,128)}, u32[]{:S(2)}) copy-start(f32[5,1024]{1,0:T(8,128)} %param.26) | copy-start | bytes 61444
  153.6 9.2 %copy-start.6 = (bf16[8,3,1024]{2,0,1:T(8,128)(2,1)S(1)}, bf16[8,3,1024]{2,0,1:T(8,128)(2,1)}, u32[]{:S(2)}) copy-start(bf16[8,3,1024]{2,0,1:T(8,128)(2,1)} %param.31) | copy-start | bytes 147460
  153.6 9.3 %copy-start.2 = (bf16[4,8,4096]{2,1,0:T(8,128)(2,1)S(1)}, bf16[4,8,4096]{2,1,0:T(8,128)(2,1)}, u32[]{:S(2)}) copy-start(bf16[4,8,4096]{2,1,0:T(8,128)(2,1)} %param.19) | copy-start | bytes 786436
  153.6 9.5 %copy-start.5 = (f32[4096]{0:T(1024)S(1)}, f32[4096]{0:T(1024)}, u32[]{:S(2)}) copy-start(f32[4096]{0:T(1024)} %param.20) | copy-start | bytes 49156
  153.7 24.1 %copy-start.3 = (bf16[4096,16]{0,1:T(8,128)(2,1)S(1)}, bf16[4096,16]{0,1:T(8,128)(2,1)}, u32[]{:S(2)}) copy-start(bf16[4096,16]{0,1:T(8,128)(2,1)} %param.25) | copy-start | bytes 393220
  153.7 24.1 %copy-start.11 = (f32[16]{0:T(128)S(1)}, f32[16]{0:T(128)}, u32[]{:S(2)}) copy-start(f32[16]{0:T(128)} %param.29) | copy-start | bytes 196
  153.7 24.1 %copy-start.12 = (f32[16]{0:T(128)S(1)}, f32[16]{0:T(128)}, u32[]{:S(2)}) copy-start(f32[16]{0:T(128)} %param.28) | copy-start | bytes 196
  378.5 13.4 %copy-start.9 = (f32[16]{0:T(128)S(1)}, f32[16]{0:T(128)}, u32[]{:S(2)}) copy-start(f32[16]{0:T(128)} %param.30) | copy-start | bytes 196
  378.5 30.2 %copy-start.4 = (f32[1024]{0:T(1024)S(1)}, f32[1024]{0:T(1024)}, u32[]{:S(2)}) copy-start(f32[1024]{0:T(1024)} %param.34) | copy-start | bytes 12292
  645.5 3.4 copy-start.1
Sparse Core Ops, SparseCore 0:
  12.7 90.1 all-gather.4
  162.9 156.2 all-gather.2
where the time goes:
time: 721 us; the launch traced here: 713 us
  blocking collectives  224 us (31%)
  waiting for transfers between devices  210 us (29%)
  matrix products  113 us (16%)
  local copies, waits for them, and re-layouts  81.8 us (11%)
  other arithmetic  63.1 us (9%)
  between operations  14.8 us (2%)
    all_gather x1, waiting for transfers between devices, body(): lax.all_gather(zx_delta.astype(jnp.bfloat16), 'dp', axis=0, tiled=True)  131 us
    psum x4, blocking collectives, body(): whole = lax.psum(partial_value, 'tp').astype(jnp.bfloat16)  109 us
    all_to_all x1, waiting for transfers between devices, body(): lax.all_to_all(zx_codes, 'tp', split_axis=2, concat_axis=0, tiled=True)  79.2 us
    psum x4, blocking collectives, body(): totals = lax.psum(squares[:, None] * group_mask, 'tp')  58.1 us
    all_gather x4, blocking collectives, body(): bc_all = lax.all_gather(conv_piece, 'tp', axis=1, tiled=True)  56.3 us
    dot_general x4, matrix products, body(): jnp.einsum('rhpn,rn->rhp', state, c_group, precision=lax.Precision.HIGHEST)  51.1 us
    dot_general x4, matrix products, body(): zx = jnp.dot(normed, zx_weights, preferred_element_type=jnp.float32)  40.7 us
    unnamed x30, local copies, waits for them, and re-layouts  27.7 us
  transfers between devices with their start and end apart: 3, of which 2 were waited for; matrix products, arithmetic and copies ran while one was open for 11% of the time, Pallas kernels for 0%

commit v1 on v0

--- a/solution.py
+++ b/solution.py
@@ -55,7 +55,10 @@
 ):
     slot = lax.axis_index("tp")
     tp_count = lax.axis_size("tp")
-    traded = lax.all_to_all(zx_codes, "tp", split_axis=2, concat_axis=0, tiled=True)
+    traded = jnp.concatenate(
+        lax.all_to_all(jnp.stack(jnp.split(zx_codes, lax.axis_size("tp"), axis=2)), "tp", 0, 0),
+        axis=0,
+    )
     zx_delta = decode_pairs(traded, zx_exponents, BLK)
     local_cols = traded.shape[2]
     gathered = lax.all_gather(zx_delta.astype(jnp.bfloat16), "dp", axis=0, tiled=True)

time: 721 us -> 696 us (0.965)
  local copies, waits for them, and re-layouts: 81.8 us -> 67.6 us
  other arithmetic: 63.1 us -> 53.8 us
    convert_element_type x1 -> x0, local copies, waits for them, and re-layouts: 17.1 us -> none  [decode_pairs(): codes.astype(jnp.float32)]
    convert_element_type x1 -> x0, other arithmetic: 8.47 us -> none  [decode_pairs(): codes.astype(jnp.float32)]
    unnamed x30 -> x36, local copies, waits for them, and re-layouts: 27.7 us -> 28.5 us
  transfers between devices with their start and end apart: 3 -> 3, of which waited for: 2 -> 2; matrix products, arithmetic and copies ran while one was open for 11% -> 8% of each run, Pallas kernels for 0% -> 0%
where the time goes in v1:
time: 696 us; the launch traced here: 689 us
  blocking collectives  224 us (32%)
  waiting for transfers between devices  210 us (30%)
  matrix products  113 us (16%)
  local copies, waits for them, and re-layouts  67.6 us (10%)
  other arithmetic  53.8 us (8%)
  between operations  14.8 us (2%)
    all_gather x1, waiting for transfers between devices, body(): lax.all_gather(zx_delta.astype(jnp.bfloat16), 'dp', axis=0, tiled=True)  131 us
    psum x4, blocking collectives, body(): whole = lax.psum(partial_value, 'tp').astype(jnp.bfloat16)  109 us
    all_to_all x1, waiting for transfers between devices, body(): lax.all_to_all(jnp.stack(jnp.split(zx_codes, lax.axis_size('tp'), axis=2)...  79.2 us
    psum x4, blocking collectives, body(): totals = lax.psum(squares[:, None] * group_mask, 'tp')  58.1 us
    all_gather x4, blocking collectives, body(): bc_all = lax.all_gather(conv_piece, 'tp', axis=1, tiled=True)  56.3 us
    dot_general x4, matrix products, body(): jnp.einsum('rhpn,rn->rhp', state, c_group, precision=lax.Precision.HIGHEST)  51.1 us
    dot_general x4, matrix products, body(): zx = jnp.dot(normed, zx_weights, preferred_element_type=jnp.float32)  40.7 us
    unnamed x36, local copies, waits for them, and re-layouts  28.5 us
  transfers between devices with their start and end apart: 3, of which 2 were waited for; matrix products, arithmetic and copies ran while one was open for 8% of the time, Pallas kernels for 0%

profile of v1, /device:TPU:0, one launch (start us, length us, event | category | flops | bytes accessed | tf_op | source)
XLA Modules:
  0.0 688.9 jit_solution(703670501271488166)
XLA Ops:
  7.2 0.8 multiply_exponential_fusion.4
  8.1 0.3 mul.639
  8.4 4.1 fusion.3
  12.6 2.2 bitcast_dynamic-update-slice_fusion.7
  14.8 2.2 bitcast_dynamic-update-slice_fusion.6
  17.1 2.2 bitcast_dynamic-update-slice_fusion.5
  19.2 2.2 bitcast_dynamic-update-slice_fusion.4
  21.4 2.3 bitcast_dynamic-update-slice_fusion.3
  23.8 2.3 bitcast_dynamic-update-slice_fusion.2
  26.0 2.3 bitcast_dynamic-update-slice_fusion.1
  28.4 2.2 bitcast_dynamic-update-slice_fusion
  30.6 6.2 all-to-all-start
  36.8 4.0 mul.609
  40.8 10.8 %mul.610 = f32[1024,2,1024]{2,1,0:T(2,128)} reshape(f32[8,128,2,8,128]{4,3,2,1,0:T(8,128)} %mul.609) | data formatting | bytes 16777216 | tf_op jit(solution)/shard_map/mul | solution.py:19
  51.7 79.2 %all-to-all-done = bf16[8,128,2,1024]{3,2,1,0:T(2,128)(2,1)} async-done(((bf16[8,128,2,1024]{3,2,1,0:T(2,128)(2,1)}), bf16[8,128,2,1024]{3,2,1,0:T(2,128)(2,1)}, u32[]{:S(2)}, u32[]{:S(2)}) %all-to-all-start) | async-done | bytes 4194336 | tf_op jit(solution)/shard_map/all_to_all | solution.py:59
  130.8 8.1 %fusion = bf16[1024,2,1024]{2,1,0:T(2,128)(2,1)} fusion(f32[1024,2,1024]{2,1,0:T(2,128)} %mul.610, bf16[8,128,2,1024]{3,2,1,0:T(2,128)(2,1)} %all-to-all-done), kind=kLoop, calls=%fused_computation.3 | loop fusion | flops 6291456 | bytes 16777216 | tf_op jit(solution)/shard_map/convert_element_type | solution.py:64
  139.2 0.1 fusion.13
  139.4 0.4 convolution_bitcast_fusion.3
  139.8 14.2 %all_gather.19 = f32[8,2048]{1,0:T(8,128)S(1)} all-gather(f32[8,256]{1,0:T(8,128)S(1)} %divide_multiply_fusion.7), channel_id=1, replica_groups=mesh['dp'=4,'tp'=8] {'tp'}, dimensions={1}, use_global_device_ids=true | all-gather | bytes 73728 | tf_op jit(solution)/shard_map/all_gather | solution.py:98
  154.0 0.2 multiply_exponential_fusion.5
  154.3 10.1 %add_convert_fusion.1 = bf16[1024,4096]{1,0:T(8,128)(2,1)} fusion(bf16[1024,4096]{1,0:T(8,128)(2,1)} %all-gather.5.cloned.1.call-done, bf16[1024,4096]{1,0:T(8,128)(2,1)} %param.35), kind=kLoop, calls=%fused_computation.1 | loop fusion | flops 16777216 | bytes 25165824 | tf_op jit(solution)/shard_map/convert_element_type | solution.py:72
  164.4 131.0 %all-gather.3.cloned.1.call-done = bf16[4096,2,1024]{2,1,0:T(2,128)(2,1)} async-done(((bf16[1024,2,1024]{2,1,0:T(2,128)(2,1)}), bf16[4096,2,1024]{2,1,0:T(2,128)(2,1)}) %all-gather.3.cloned.1.call-update) | async-done | bytes 16777232 | tf_op jit(solution)/shard_map/all_gather | solution.py:64
  295.4 19.2 %add_convert_fusion = bf16[4096,2,1024]{2,1,0:T(2,128)(2,1)S(1)} fusion(bf16[4096,2,1024]{2,1,0:T(2,128)(2,1)} %all-gather.3.cloned.1.call-done, bf16[4096,2,1024]{2,1,0:T(2,128)(2,1)} %param.21), kind=kLoop, calls=%fused_computation | loop fusion | flops 33554432 | bytes 50331648 | tf_op jit(solution)/shard_map/convert_element_type | solution.py:67
  314.6 9.3 %copy.32 = bf16[512,8,2,1024]{3,1,2,0:T(8,128)(2,1)} copy(bf16[512,8,2,1024]{3,2,1,0:T(2,128)(2,1)S(1)} %bitcast.221) | data formatting | bytes 33554432
  323.9 20.7 %copy.23 = bf16[2048,4096]{1,0:T(8,128)(2,1)} copy(bf16[2048,4096]{0,1:T(8,128)(2,1)} %bitcast.222) | data formatting | bytes 33554432 | tf_op jit(solution)/shard_map/dot_general | solution.py:90
  344.6 10.2 %fusion.29 = f32[8,2,1024]{2,0,1:T(8,128)S(1)} fusion(bf16[2,1024,4096]{2,1,0:T(8,128)(2,1)} %bitcast.217, f32[4096]{0:T(1024)S(1)} %copy-done.5, f32[8]{0:T(128)S(1)} %add_rsqrt_fusion.7, bf16[4,8,4096]{2,1,0:T(8,128)(2,1)S(1)} %copy-done.2), kind=kOutput, calls=%fused_computation.74 | convolution fusion | flops 134348800 | bytes 16925184 | tf_op jit(solution)/shard_map/dot_general | solution.py:90
  355.1 13.1 %fusion.1 = f32[8,1,16,64]{3,1,2,0:T(1,128)S(1)} fusion(f32[8,16,64,256]{3,2,1,0:T(8,128)} %param.33, f32[8,256]{1,0:T(8,128)S(1)} %get-tuple-element.23, f32[8,16,64]{2,1,0:T(8,128)S(1)} %broadcast_multiply_fusion.3, f32[8,16]{1,0:T(8,128)S(1)} %get-tuple-element.26, f32[8,256,1,1]{1,0,2,3:T(8,128)S(1)} %get-tuple-element.22), kind=kOutput, calls=%fused_computation.8 | convolution fusion | flops 31457280 | bytes 8471040 | tf_op jit(solution)/shard_map/rhpn,rn->rhp/dot_general | solution.py:109
  368.1 0.2 multiply_reduce_fusion.6
  368.4 16.4 %psum.56 = f32[8,4]{0,1:T(4,128)S(1)} all-reduce(f32[8,4]{0,1:T(4,128)S(1)} %broadcast_multiply_fusion.7), channel_id=1, replica_groups=mesh['dp'=4,'tp'=8] {'tp'}, use_global_device_ids=true, to_apply=%region_4.5 | all-reduce | flops 32 | bytes 256 | tf_op jit(solution)/shard_map/psum | solution.py:114
  385.0 4.6 fusion.84
  389.6 27.1 %all-reduce.4 = bf16[8,4096]{1,0:T(8,128)(2,1)S(1)} all-reduce(f32[8,4096]{1,0:T(8,128)S(1)} %fusion.84), channel_id=1, replica_groups=mesh['dp'=4,'tp'=8] {'tp'}, use_global_device_ids=true, to_apply=%region_6.7 | all-reduce | flops 32768 | bytes 196608 | tf_op jit(solution)/shard_map/psum | solution.py:118
  416.8 0.1 multiply_reduce_fusion.2
  417.0 10.2 %fusion.35 = f32[8,2,1024]{2,0,1:T(8,128)S(1)} fusion(bf16[2,1024,4096]{2,1,0:T(8,128)(2,1)} %bitcast.218, bf16[8,4096]{1,0:T(8,128)(2,1)S(1)} %multiply_convert_fusion.2), kind=kOutput, calls=%fused_computation.79 | convolution fusion | flops 134217728 | bytes 16908288 | tf_op jit(solution)/shard_map/dot_general | solution.py:90
  427.3 0.2 multiply_exponential_fusion.3
  427.4 0.4 convolution_bitcast_fusion.2
  427.9 14.0 %all_gather.21 = f32[8,2048]{1,0:T(8,128)S(1)} all-gather(f32[8,256]{1,0:T(8,128)S(1)} %divide_multiply_fusion.6), channel_id=1, replica_groups=mesh['dp'=4,'tp'=8] {'tp'}, dimensions={1}, use_global_device_ids=true | all-gather | bytes 73728 | tf_op jit(solution)/shard_map/all_gather | solution.py:98
  442.1 13.7 %fusion.10 = f32[8,1,16,64]{3,1,2,0:T(1,128)S(1)} fusion(f32[8,16,64,256]{3,2,1,0:T(8,128)} %param.33, f32[8,256]{1,0:T(8,128)S(1)} %get-tuple-element.19, f32[8,16,64]{2,1,0:T(8,128)S(1)} %broadcast_multiply_fusion.2, f32[8,16]{1,0:T(8,128)S(1)} %get-tuple-element.28, f32[8,256]{1,0:T(8,128)S(1)} %get-tuple-element.23, ...), kind=kOutput, calls=%fused_computation.18 | convolution fusion | flops 37748736 | bytes 8512512 | tf_op jit(solution)/shard_map/rhpn,rn->rhp/dot_general | solution.py:109
  455.8 0.2 multiply_reduce_fusion.5
  456.1 13.9 %psum.58 = f32[8,4]{0,1:T(4,128)S(1)} all-reduce(f32[8,4]{0,1:T(4,128)S(1)} %broadcast_multiply_fusion.6), channel_id=1, replica_groups=mesh['dp'=4,'tp'=8] {'tp'}, use_global_device_ids=true, to_apply=%region_11.12 | all-reduce | flops 32 | bytes 256 | tf_op jit(solution)/shard_map/psum | solution.py:114
  470.2 4.6 fusion.82
  474.8 27.7 %all-reduce.5 = bf16[8,4096]{1,0:T(8,128)(2,1)S(1)} all-reduce(f32[8,4096]{1,0:T(8,128)S(1)} %fusion.82), channel_id=1, replica_groups=mesh['dp'=4,'tp'=8] {'tp'}, use_global_device_ids=true, to_apply=%region_13.14 | all-reduce | flops 32768 | bytes 196608 | tf_op jit(solution)/shard_map/psum | solution.py:118
  502.5 0.1 multiply_reduce_fusion.1
  502.7 10.2 %fusion.33 = f32[8,2,1024]{2,0,1:T(8,128)S(1)} fusion(bf16[2,1024,4096]{2,1,0:T(8,128)(2,1)} %bitcast.219, bf16[8,4096]{1,0:T(8,128)(2,1)S(1)} %multiply_convert_fusion.1), kind=kOutput, calls=%fused_computation.77 | convolution fusion | flops 134217728 | bytes 16908288 | tf_op jit(solution)/shard_map/dot_general | solution.py:90
  513.0 0.2 multiply_exponential_fusion.2
  513.1 0.4 convolution_bitcast_fusion.1
  513.6 14.0 %all_gather.22 = f32[8,2048]{1,0:T(8,128)S(1)} all-gather(f32[8,256]{1,0:T(8,128)S(1)} %divide_multiply_fusion.5), channel_id=1, replica_groups=mesh['dp'=4,'tp'=8] {'tp'}, dimensions={1}, use_global_device_ids=true | all-gather | bytes 73728 | tf_op jit(solution)/shard_map/all_gather | solution.py:98
  527.8 14.5 %fusion.2 = f32[8,1,16,64]{3,1,2,0:T(1,128)S(1)} fusion(f32[8,256]{1,0:T(8,128)S(1)} %get-tuple-element.15, f32[8,16,64]{2,1,0:T(8,128)S(1)} %broadcast_multiply_fusion.1, f32[8,16]{1,0:T(8,128)S(1)} %get-tuple-element.30, f32[8,16,64,256]{3,2,1,0:T(8,128)} %param.33, f32[8,256]{1,0:T(8,128)S(1)} %get-tuple-element.19, ...), kind=kOutput, calls=%fused_computation.9 | convolution fusion | flops 44040192 | bytes 8553984 | tf_op jit(solution)/shard_map/rhpn,rn->rhp/dot_general | solution.py:109
  542.3 0.2 multiply_reduce_fusion.4
  542.6 13.9 %psum.60 = f32[8,4]{0,1:T(4,128)S(1)} all-reduce(f32[8,4]{0,1:T(4,128)S(1)} %broadcast_multiply_fusion.5), channel_id=1, replica_groups=mesh['dp'=4,'tp'=8] {'tp'}, use_global_device_ids=true, to_apply=%region_18.19 | all-reduce | flops 32 | bytes 256 | tf_op jit(solution)/shard_map/psum | solution.py:114
  556.7 4.6 fusion.80
  561.3 27.2 %all-reduce.6 = bf16[8,4096]{1,0:T(8,128)(2,1)S(1)} all-reduce(f32[8,4096]{1,0:T(8,128)S(1)} %fusion.80), channel_id=1, replica_groups=mesh['dp'=4,'tp'=8] {'tp'}, use_global_device_ids=true, to_apply=%region_20.21 | all-reduce | flops 32768 | bytes 196608 | tf_op jit(solution)/shard_map/psum | solution.py:118
  588.6 0.1 multiply_reduce_fusion
  588.8 10.2 %fusion.31 = f32[8,2,1024]{2,0,1:T(8,128)S(1)} fusion(bf16[2,1024,4096]{2,1,0:T(8,128)(2,1)} %bitcast.220, bf16[8,4096]{1,0:T(8,128)(2,1)S(1)} %multiply_convert_fusion), kind=kOutput, calls=%fused_computation.75 | convolution fusion | flops 134217728 | bytes 16908288 | tf_op jit(solution)/shard_map/dot_general | solution.py:90
  599.0 0.2 multiply_exponential_fusion.1
  599.2 0.4 convolution_bitcast_fusion
  599.7 14.2 %all_gather.23 = f32[8,2048]{1,0:T(8,128)S(1)} all-gather(f32[8,256]{1,0:T(8,128)S(1)} %divide_multiply_fusion.4), channel_id=1, replica_groups=mesh['dp'=4,'tp'=8] {'tp'}, dimensions={1}, use_global_device_ids=true | all-gather | bytes 73728 | tf_op jit(solution)/shard_map/all_gather | solution.py:98
  614.1 7.7 %multiply_add_fusion = f32[8,16,64,256]{3,2,1,0:T(8,128)S(1)} fusion(f32[8,256]{1,0:T(8,128)S(1)} %get-tuple-element.11, f32[8,16,64]{2,1,0:T(8,128)S(1)} %broadcast_multiply_fusion, f32[8,16]{1,0:T(8,128)S(1)} %get-tuple-element.32, f32[8,256]{1,0:T(8,128)S(1)} %get-tuple-element.15, f32[8,16,64]{2,1,0:T(8,128)S(1)} %broadcast_multiply_fusion.1, ...), kind=kLoop, calls=%fused_computation.4 | loop fusion | flops 25165824 | bytes 16943104 | tf_op jit(solution)/shard_map/add | solution.py:105
  621.8 3.4 copy-done.1
  625.2 9.8 %fusion.99 = f32[8,1,16,64]{3,1,2,0:T(1,128)S(1)} fusion(f32[8,16,64,256]{3,2,1,0:T(8,128)S(1)} %multiply_add_fusion, f32[8,256,1,1]{1,0,2,3:T(8,128)S(1)} %get-tuple-element.10), kind=kOutput, calls=%fused_computation.179 | convolution fusion | flops 25165824 | bytes 8429568 | tf_op jit(solution)/shard_map/rhpn,rn->rhp/dot_general | solution.py:109
  635.0 0.2 multiply_reduce_fusion.3
  635.3 13.9 %psum.62 = f32[8,4]{0,1:T(4,128)S(1)} all-reduce(f32[8,4]{0,1:T(4,128)S(1)} %broadcast_multiply_fusion.4), channel_id=1, replica_groups=mesh['dp'=4,'tp'=8] {'tp'}, use_global_device_ids=true, to_apply=%region_25.26 | all-reduce | flops 32 | bytes 256 | tf_op jit(solution)/shard_map/psum | solution.py:114
  649.4 4.6 fusion.78
  654.0 27.2 %all-reduce.7 = bf16[8,4096]{1,0:T(8,128)(2,1)S(1)} all-reduce(f32[8,4096]{1,0:T(8,128)S(1)} %fusion.78), channel_id=1, replica_groups=mesh['dp'=4,'tp'=8] {'tp'}, use_global_device_ids=true, to_apply=%region_27.28 | all-reduce | flops 32768 | bytes 196608 | tf_op jit(solution)/shard_map/psum | solution.py:118
  681.3 0.6 pad_maximum_fusion.6
  (106 shorter events, 2.9 us)
Async XLA Ops:
  7.2 132.2 %copy-start = (bf16[4096,256]{1,0:T(8,128)(2,1)S(1)}, bf16[4096,256]{1,0:T(8,128)(2,1)}, u32[]{:S(2)}) copy-start(bf16[4096,256]{1,0:T(8,128)(2,1)} %param.24) | copy-start | bytes 6291460
  7.2 147.1 %all-gather.5.cloned.1.call-start = ((), (), s32[]{:S(2)}) async-start(), calls=%async_computation.2 | async-start | bytes 10485760 | tf_op jit(solution)/shard_map/all_gather | solution.py:71
  12.6 24.2 %copy-start.10 = (s32[8,2,8]{2,1,0:T(2,128)S(1)}, s32[8,2,8]{2,1,0:T(2,128)}, u32[]{:S(2)}) copy-start(s32[8,2,8]{2,1,0:T(2,128)} %param.23) | copy-start | bytes 1540
  30.6 100.3 %all-to-all-start = ((bf16[8,128,2,1024]{3,2,1,0:T(2,128)(2,1)}), bf16[8,128,2,1024]{3,2,1,0:T(2,128)(2,1)}, u32[]{:S(2)}, u32[]{:S(2)}) async-start(bf16[8,128,2,1024]{3,2,1,0:T(2,128)(2,1)} %bitcast_dynamic-update-slice_fusion), calls=%async_computation | async-start | bytes 8388608 | tf_op jit(solution)/shard_map/all_to_all | solution.py:59
  36.8 258.6 %all-gather.3.cloned.1.call-start = ((), (), s32[]{:S(2)}) async-start(), calls=%async_computation.1 | async-start | bytes 20971520 | tf_op jit(solution)/shard_map/all_gather | solution.py:64
  51.6 87.4 %copy-start.13 = (f32[5,256]{1,0:T(8,128)S(1)}, f32[5,256]{1,0:T(8,128)}, u32[]{:S(2)}) copy-start(f32[5,256]{1,0:T(8,128)} %param.27) | copy-start | bytes 15364
  51.6 87.4 %copy-start.8 = (bf16[8,3,256]{2,0,1:T(8,128)(2,1)S(1)}, bf16[8,3,256]{2,0,1:T(8,128)(2,1)}, u32[]{:S(2)}) copy-start(bf16[8,3,256]{2,0,1:T(8,128)(2,1)} %param.32) | copy-start | bytes 36868
  51.6 87.5 %copy-start.7 = (f32[5,1024]{1,0:T(8,128)S(1)}, f32[5,1024]{1,0:T(8,128)}, u32[]{:S(2)}) copy-start(f32[5,1024]{1,0:T(8,128)} %param.26) | copy-start | bytes 61444
  51.6 87.5 %copy-start.6 = (bf16[8,3,1024]{2,0,1:T(8,128)(2,1)S(1)}, bf16[8,3,1024]{2,0,1:T(8,128)(2,1)}, u32[]{:S(2)}) copy-start(bf16[8,3,1024]{2,0,1:T(8,128)(2,1)} %param.31) | copy-start | bytes 147460
  51.6 87.6 %copy-start.2 = (bf16[4,8,4096]{2,1,0:T(8,128)(2,1)S(1)}, bf16[4,8,4096]{2,1,0:T(8,128)(2,1)}, u32[]{:S(2)}) copy-start(bf16[4,8,4096]{2,1,0:T(8,128)(2,1)} %param.19) | copy-start | bytes 786436
  51.6 87.7 %copy-start.5 = (f32[4096]{0:T(1024)S(1)}, f32[4096]{0:T(1024)}, u32[]{:S(2)}) copy-start(f32[4096]{0:T(1024)} %param.20) | copy-start | bytes 49156
  51.6 102.4 %copy-start.3 = (bf16[4096,16]{0,1:T(8,128)(2,1)S(1)}, bf16[4096,16]{0,1:T(8,128)(2,1)}, u32[]{:S(2)}) copy-start(bf16[4096,16]{0,1:T(8,128)(2,1)} %param.25) | copy-start | bytes 393220
  51.7 102.4 %copy-start.11 = (f32[16]{0:T(128)S(1)}, f32[16]{0:T(128)}, u32[]{:S(2)}) copy-start(f32[16]{0:T(128)} %param.29) | copy-start | bytes 196
  51.7 102.4 %copy-start.12 = (f32[16]{0:T(128)S(1)}, f32[16]{0:T(128)}, u32[]{:S(2)}) copy-start(f32[16]{0:T(128)} %param.28) | copy-start | bytes 196
  354.7 13.4 %copy-start.9 = (f32[16]{0:T(128)S(1)}, f32[16]{0:T(128)}, u32[]{:S(2)}) copy-start(f32[16]{0:T(128)} %param.30) | copy-start | bytes 196
  354.7 30.2 %copy-start.4 = (f32[1024]{0:T(1024)S(1)}, f32[1024]{0:T(1024)}, u32[]{:S(2)}) copy-start(f32[1024]{0:T(1024)} %param.34) | copy-start | bytes 12292
  621.8 3.4 copy-start.1
Sparse Core Ops, SparseCore 0:
  12.7 90.1 all-gather.4
  139.1 156.2 all-gather.2
